TPU v7x, 32 devices: a whole 2x2x4 slice. The times are simulated.
32 devices in a mesh: ctx: 4 (over y, x), tp: 8 (over z, core).
Axes of the slice: x: 2, y: 2, z: 4, core: 2. Of those that a mesh axis runs over, the one named last changes fastest.
Arguments:
- tokens: bfloat16 [3072, 8192], P('ctx', 'tp'), may hold values from -6 to 6
- w_in: bfloat16 [8192, 3, 4096], P(None, None, 'tp'), may hold values from -0.0625 to 0.0625
- short_taps: bfloat16 [3, 3, 4096], P(None, None, 'tp'), may hold values from -3 to 3
- long_taps: bfloat16 [128, 4096], P(None, 'tp'), may hold values from -0.5 to 0.5
- skip_gain: float32 [4096], P('tp'), may hold values from 0.5 to 1.5
- w_out: bfloat16 [4096, 8192], P('tp'), may hold values from -0.125 to 0.125
Outputs:
- mixed: bfloat16 [3072, 8192], P('ctx', 'tp')
All inputs are finite; a program needn't handle non-finite values.
Results may differ from a plain program's by a relative error of at most 0.014.
Values may be sent and summed in bfloat16 or wider, within the bound.
No kernel may reach another device: no remote copies, remote signals or barrier semaphores. Data moves between devices by JAX's collectives and lax.ppermute only.
A program may use at most 256 MiB of HBM per device.

v0:
```python
import jax
import jax.numpy as jnp
from jax import lax
from jax.sharding import PartitionSpec as P

FILT = 128
SHORT = 3


def from_behind(value, axis, steps):
    count = lax.axis_size(axis)
    first, last = (max(0, -steps), min(count, count - steps))
    return lax.ppermute(value, axis, [(source, source + steps) for source in range(first, last)])


def short_mix(extended, count, taps):
    total = jnp.zeros((count,) + extended.shape[1:], jnp.float32)
    for k in range(SHORT):
        begin = SHORT - 1 - k
        total = total + taps[:, k, :][None] * extended[begin : begin + count].astype(jnp.float32)
    return total


def toeplitz_blocks(long_taps):
    local = long_taps.shape[1]
    column = jnp.concatenate(
        [
            jnp.zeros((1, local), long_taps.dtype),
            jnp.flip(long_taps, axis=0),
            jnp.zeros((FILT, local), long_taps.dtype),
        ],
        axis=0,
    )
    spread = jnp.broadcast_to(column[None], (FILT, 2 * FILT + 1, local)).reshape(
        FILT * (2 * FILT + 1), local
    )
    return spread[: FILT * 2 * FILT].reshape(FILT, 2 * FILT, local)


def body(tokens, w_in, short_taps, long_taps, skip_gain, w_out):
    rows = tokens.shape[0]
    width = w_in.shape[0]
    local = w_in.shape[2]
    flat_weight = w_in.reshape(width, 3 * local)
    projected = jnp.dot(
        lax.all_gather(tokens, "tp", axis=1, tiled=True),
        flat_weight,
        preferred_element_type=jnp.float32,
    )
    u_low = lax.optimization_barrier(projected.astype(jnp.bfloat16)).reshape(rows, 3, local)
    taps = short_taps.astype(jnp.float32)
    short_edge = from_behind(u_low[rows - (SHORT - 1) :], "ctx", 1)
    mixed_short = short_mix(jnp.concatenate([short_edge, u_low], axis=0), rows, taps)
    z_low = (mixed_short[:, 1] * mixed_short[:, 2]).astype(jnp.bfloat16)
    z_edge = from_behind(z_low[rows - (FILT - 1) :], "ctx", 1)
    z_joined = jnp.concatenate([jnp.zeros((1, local), jnp.bfloat16), z_edge, z_low], axis=0)
    blocks = z_joined.reshape(rows // FILT + 1, FILT, local)
    windows = jnp.concatenate([blocks[:-1], blocks[1:]], axis=1)
    matrix = toeplitz_blocks(long_taps)
    filtered = jnp.einsum(
        "isc,bsc->bic", matrix, windows, preferred_element_type=jnp.float32
    ).reshape(rows, local)
    filtered = filtered + skip_gain[None] * z_low.astype(jnp.float32)
    gated = (mixed_short[:, 0] * filtered).astype(jnp.bfloat16)
    terms = jnp.dot(gated, w_out, preferred_element_type=jnp.float32)
    result = lax.psum_scatter(terms.astype(jnp.bfloat16), "tp", scatter_dimension=1, tiled=True)
    return result


def solution(mesh):
    in_specs = (
        P("ctx", "tp"),
        P(None, None, "tp"),
        P(None, None, "tp"),
        P(None, "tp"),
        P("tp"),
        P("tp", None),
    )
    out_specs = P("ctx", "tp")
    return jax.shard_map(body, mesh=mesh, in_specs=in_specs, out_specs=out_specs, check_vma=False)
```

profile of v0, /device:TPU:0, one launch (start us, length us, event | category | flops | bytes accessed | tf_op | source)
XLA Modules:
  0.0 457.2 jit_solution(14925680088055711178)
XLA Ops:
  6.5 0.0 all-gather.2.cloned.1.call-start
  6.5 0.7 all-gather.2.cloned.1.call-update
  7.3 0.0 copy-start.4
  7.3 0.0 reduce-scatter.2.cloned.1.call-start
  7.3 32.1 %copy.13 = bf16[8192,3,512]{0,2,1:T(8,128)(2,1)} copy(bf16[8192,3,512]{2,0,1:T(8,128)(2,1)} %param.7) | data formatting | bytes 50331648 | tf_op args[1]
  39.4 0.0 copy-done.4
  39.4 89.0 %all-gather.2.cloned.1.call-done = bf16[768,8192]{1,0:T(8,128)(2,1)} async-done(((bf16[768,1024]{1,0:T(8,128)(2,1)}), bf16[768,8192]{1,0:T(8,128)(2,1)}) %all-gather.2.cloned.1.call-update) | async-done | bytes 12582928 | tf_op jit(solution)/shard_map/all_gather | solution.py:46
  128.4 0.0 copy-start.2
  128.4 24.4 %convolution_convert_fusion.1 = bf16[768,1536]{1,0:T(8,128)(2,1)S(1)} fusion(bf16[768,8192]{1,0:T(8,128)(2,1)} %all-gather.2.cloned.1.call-done, bf16[8192,1536]{0,1:T(8,128)(2,1)} %bitcast.36), kind=kOutput, calls=%fused_computation.2 | convolution fusion | flops 19328532480 | bytes 40108032 | tf_op jit(solution)/shard_map/dot_general | solution.py:45
  152.8 0.0 copy-start.1
  152.8 1.4 copy-done.1
  154.2 0.3 copy.25
  154.5 3.4 collective-permute-start
  157.9 0.0 copy-done.2
  157.9 0.2 rev.4
  158.1 0.1 pad.2.clone
  158.2 2.8 copy.14
  161.0 5.6 %collective-permute-done = bf16[2,3,512]{0,2,1:T(8,128)(2,1)S(1)} collective-permute-done((bf16[2,3,512]{0,2,1:T(8,128)(2,1)S(1)}, bf16[2,3,512]{0,2,1:T(8,128)(2,1)S(1)}, u32[]{:S(2)}, u32[]{:S(2)}) %collective-permute-start) | collective-permute-done | bytes 6176 | tf_op jit(solution)/shard_map/ppermute | solution.py:13
  166.6 3.0 multiply_add_fusion
  169.7 0.0 copy-start
  169.7 2.2 copy-done
  171.9 0.1 fusion.8
  172.0 0.1 slice_bitcast_fusion.1
  172.1 4.6 %collective-permute-start.1 = (bf16[127,512]{0,1:T(8,128)(2,1)S(1)}, bf16[127,512]{0,1:T(8,128)(2,1)S(1)}, u32[]{:S(2)}, u32[]{:S(2)}) collective-permute-start(bf16[127,512]{0,1:T(8,128)(2,1)S(1)} %slice_bitcast_fusion.1), channel_id=1, source_target_pairs={{0,8},{8,16},{16,24},{1,9},{9,17},{17,25},{2,10},{10,18},{18,26},{... | collective-permute-start | bytes 390152 | tf_op jit(solution)/shard_map/ppermute | solution.py:13
  176.7 0.1 maximum_maximum_fusion
  176.8 11.6 %broadcast_in_dim.5 = bf16[128,257,512]{2,1,0:T(8,128)(2,1)} broadcast(bf16[257,512]{1,0:T(8,128)(2,1)S(1)} %maximum_maximum_fusion), dimensions={1,2} | broadcast | bytes 33948672 | tf_op jit(solution)/shard_map/broadcast_in_dim | solution.py:34
  188.4 30.6 %reshape.33 = bf16[32896,512]{1,0:T(8,128)(2,1)} reshape(bf16[128,257,512]{2,1,0:T(8,128)(2,1)} %broadcast_in_dim.5) | data formatting | bytes 67371008 | tf_op jit(solution)/shard_map/reshape | solution.py:34
  219.0 22.8 %slice.72 = bf16[32768,512]{1,0:T(8,128)(2,1)} slice(bf16[32896,512]{1,0:T(8,128)(2,1)} %reshape.33), slice={[0:32768], [0:512]} | slice | bytes 67108864 | tf_op jit(solution)/shard_map/slice | solution.py:37
  241.9 45.7 %copy.26 = bf16[128,256,512]{1,0,2:T(8,128)(2,1)} copy(bf16[128,256,512]{2,1,0:T(8,128)(2,1)} %bitcast.35) | data formatting | bytes 67108864 | tf_op jit(solution)/shard_map/reshape | solution.py:37
  287.5 0.3 copy.16
  287.8 1.5 copy.20
  289.3 0.0 collective-permute-done.1
  289.3 0.1 copy.17
  289.4 0.1 pad_maximum_fusion.1
  289.5 1.5 copy.19
  291.0 14.9 %fusion.5 = f32[6,128,512]{1,0,2:T(8,128)S(1)} fusion(bf16[128,256,512]{1,0,2:T(8,128)(2,1)} %copy.26, bf16[6,128,512]{1,0,2:T(8,128)(2,1)} %copy.20, bf16[6,128,512]{1,0,2:T(8,128)(2,1)} %copy.19), kind=kOutput, calls=%fused_computation.11 | convolution fusion | flops 204472320 | bytes 36700160 | tf_op jit(solution)/shard_map/isc,bsc->bic/dot_general | solution.py:60
  305.8 0.0 copy-start.3
  305.9 1.6 copy.22
  307.5 1.9 copy.24
  309.3 0.0 copy-done.3
  309.4 13.5 %convolution_convert_fusion = bf16[768,8192]{1,0:T(8,128)(2,1)} fusion(bf16[512,8192]{1,0:T(8,128)(2,1)} %param.11, f32[768,3,512]{0,2,1:T(8,128)} %copy-done, f32[768,512]{0,1:T(8,128)S(1)} %copy.24, bf16[768,1,512]{0,2,1:T(8,128)(2,1)S(1)} %fusion.8, f32[512]{0:T(512)S(1)} %copy-done.3), kind=kOutput, calls=%fused_computation | convolution fusion | flops 6450708480 | bytes 24905728 | tf_op jit(solution)/shard_map/dot_general | solution.py:65
  322.8 0.0 reduce-scatter.2.cloned.1.call-update
  322.9 127.5 %reduce-scatter.2.cloned.1.call-done = bf16[768,1024]{1,0:T(8,128)(2,1)} async-done(((bf16[768,8192]{1,0:T(8,128)(2,1)}), bf16[768,1024]{1,0:T(8,128)(2,1)}) %reduce-scatter.2.cloned.1.call-update) | async-done | bytes 1572880 | tf_op jit(solution)/shard_map/reduce_scatter | solution.py:66
  (6 shorter events, 0.0 us)
Async XLA Ops:
  6.5 121.9 %all-gather.2.cloned.1.call-start = ((), (), s32[]{:S(2)}) async-start(), calls=%async_computation.1 | async-start | bytes 14155776 | tf_op jit(solution)/shard_map/all_gather | solution.py:46
  7.3 32.1 %copy-start.4 = (bf16[3,3,512]{2,1,0:T(4,128)(2,1)S(1)}, bf16[3,3,512]{2,1,0:T(4,128)(2,1)}, u32[]{:S(2)}) copy-start(bf16[3,3,512]{2,1,0:T(4,128)(2,1)} %param.8) | copy-start | bytes 27652
  7.3 443.1 %reduce-scatter.2.cloned.1.call-start = ((), (), s32[]{:S(2)}) async-start(), calls=%async_computation.2 | async-start | bytes 14155776 | tf_op jit(solution)/shard_map/reduce_scatter | solution.py:66
  128.4 29.5 %copy-start.2 = (bf16[128,512]{1,0:T(8,128)(2,1)S(1)}, bf16[128,512]{1,0:T(8,128)(2,1)}, u32[]{:S(2)}) copy-start(bf16[128,512]{1,0:T(8,128)(2,1)} %param.9) | copy-start | bytes 393220
  152.8 1.4 copy-start.1
  154.5 12.2 %collective-permute-start = (bf16[2,3,512]{0,2,1:T(8,128)(2,1)S(1)}, bf16[2,3,512]{0,2,1:T(8,128)(2,1)S(1)}, u32[]{:S(2)}, u32[]{:S(2)}) collective-permute-start(bf16[2,3,512]{0,2,1:T(8,128)(2,1)S(1)} %bitcast.42), channel_id=1, source_target_pairs={{0,8},{8,16},{16,24},{1,9},{9,17},{17,25},{2,10},{10,18},{18,26},{... | collective-permute-start | bytes 18440 | tf_op jit(solution)/shard_map/ppermute | solution.py:13
  169.7 2.2 copy-start
  172.1 117.1 %collective-permute-start.1 = (bf16[127,512]{0,1:T(8,128)(2,1)S(1)}, bf16[127,512]{0,1:T(8,128)(2,1)S(1)}, u32[]{:S(2)}, u32[]{:S(2)}) collective-permute-start(bf16[127,512]{0,1:T(8,128)(2,1)S(1)} %slice_bitcast_fusion.1), channel_id=1, source_target_pairs={{0,8},{8,16},{16,24},{1,9},{9,17},{17,25},{2,10},{10,18},{18,26},{... | collective-permute-start | bytes 390152 | tf_op jit(solution)/shard_map/ppermute | solution.py:13
  305.8 3.5 copy-start.3
Sparse Core Ops, SparseCore 0:
  8.9 119.4 all-gather.1
  323.0 127.2 reduce-scatter.1
where the time goes:
time: 460 us; the launch traced here: 457 us
  waiting for transfers between devices  223 us (48%)
  local copies, waits for them, and re-layouts  157 us (34%)
  matrix products  52.7 us (11%)
  between operations  13.6 us (3%)
  starting transfers between devices  8.02 us (2%)
    reduce_scatter x1, waiting for transfers between devices, body(): lax.psum_scatter(terms.astype(jnp.bfloat16), 'tp', scatter_dimension=1, t...  127 us
    all_gather x1, waiting for transfers between devices, body(): lax.all_gather(tokens, 'tp', axis=1, tiled=True)  89 us
    reshape x1, local copies, waits for them, and re-layouts, toeplitz_blocks(): return spread[:FILT * 2 * FILT].reshape(FILT, 2 * FILT, local)  45.7 us
    unnamed x13, local copies, waits for them, and re-layouts  35.7 us
    reshape x1, local copies, waits for them, and re-layouts, toeplitz_blocks(): jnp.broadcast_to(column[None], (FILT, 2 * FILT + 1, local))  30.6 us
    dot_general x1, matrix products, body(): jnp.dot(lax.all_gather(tokens, 'tp', axis=1, tiled=True), flat_weight, pr...  24.4 us
    slice x1, local copies, waits for them, and re-layouts, toeplitz_blocks(): return spread[:FILT * 2 * FILT].reshape(FILT, 2 * FILT, local)  22.8 us
    dot_general x1, matrix products, body(): jnp.einsum('isc,bsc->bic', matrix, windows, preferred_element_type=jnp.fl...  14.9 us
  transfers between devices with their start and end apart: 4, of which 3 were waited for; matrix products, arithmetic and copies ran while one was open for 32% of the time, Pallas kernels for 0%

commit v1 on v0

v1 whole, which is shorter than its diff:
```python
import jax
import jax.numpy as jnp
from jax import lax
from jax.experimental import pallas as pl
from jax.experimental.pallas import tpu as pltpu
from jax.sharding import PartitionSpec as P

FILT = 128
SHORT = 3
HALO = 144
LANES = 128
F32 = jnp.float32
BF16 = jnp.bfloat16


def from_behind(value, axis, steps):
    count = lax.axis_size(axis)
    first, last = (max(0, -steps), min(count, count - steps))
    return lax.ppermute(value, axis, [(source, source + steps) for source in range(first, last)])


def mix_kernel(u0, u1, u2, short_ref, long_ref, skip_ref, g_ref, wide, shifted, taps_f):
    rows = g_ref.shape[0]
    span = rows + FILT
    tile = next(size for size in (64, 48, 32, 16) if rows % size == 0)
    taps_f[...] = long_ref[...].astype(F32)
    short = short_ref[...].astype(F32)

    def stream(j, ref, begin, count):
        total = None
        for k in range(SHORT):
            term = short[j, k : k + 1, :] * wide[j, pl.ds(begin - k, count), :]
            total = term if total is None else total + term
        return total

    for j, ref in enumerate((u0, u1, u2)):
        wide[j] = ref[...].astype(F32)
    lead = HALO - FILT
    z = (stream(1, u1, lead, span) * stream(2, u2, lead, span)).astype(BF16).astype(F32)
    shifted[0, pl.ds(0, 8), :] = jnp.zeros((8, LANES), F32)
    shifted[0, pl.ds(8, span), :] = z
    for r in range(1, 8):
        shifted[r, pl.ds(8, span), :] = shifted[0, pl.ds(8 - r, span), :]

    def one_tile(i, carry):
        begin = pl.multiple_of(i * tile, 16)
        total = jnp.zeros((tile, LANES), F32)
        for r in range(8):
            window = shifted[r, pl.ds(begin + 16, tile + FILT - 8), :]
            for q in range(FILT // 8):
                at = FILT - 8 - 8 * q
                k = 8 * q + r
                total = total + taps_f[k : k + 1, :] * window[at : at + tile]
        total = total + skip_ref[...] * shifted[0, pl.ds(begin + FILT + 8, tile), :]
        gate = None
        for k in range(SHORT):
            term = short[0, k : k + 1, :] * wide[0, pl.ds(begin + HALO - k, tile), :]
            gate = term if gate is None else gate + term
        g_ref[pl.ds(begin, tile), :] = (gate * total).astype(BF16)
        return carry

    lax.fori_loop(0, rows // tile, one_tile, 0)


def mix(extended, short_taps, long_taps, skip_gain):
    local = long_taps.shape[1]
    blocks = local // LANES
    rows = extended.shape[0] - HALO
    stream_spec = lambda j: pl.BlockSpec((HALO + rows, LANES), lambda i: (0, j * blocks + i))
    return pl.pallas_call(
        mix_kernel,
        out_shape=jax.ShapeDtypeStruct((rows, local), BF16),
        grid=(blocks,),
        in_specs=[
            stream_spec(0),
            stream_spec(1),
            stream_spec(2),
            pl.BlockSpec((3, SHORT, LANES), lambda i: (0, 0, i)),
            pl.BlockSpec((FILT, LANES), lambda i: (0, i)),
            pl.BlockSpec((1, LANES), lambda i: (0, i)),
        ],
        out_specs=pl.BlockSpec((rows, LANES), lambda i: (0, i)),
        scratch_shapes=[
            pltpu.VMEM((3, HALO + rows, LANES), F32),
            pltpu.VMEM((8, 8 + FILT + rows, LANES), F32),
            pltpu.VMEM((FILT, LANES), F32),
        ],
        cost_estimate=pl.CostEstimate(
            flops=300 * rows * local, bytes_accessed=8 * rows * local, transcendentals=0
        ),
        name="mix",
    )(extended, extended, extended, short_taps, long_taps, skip_gain[None])


def body(tokens, w_in, short_taps, long_taps, skip_gain, w_out):
    rows = tokens.shape[0]
    streams = jnp.transpose(w_in, (1, 0, 2))
    gathered = lax.all_gather(tokens, "tp", axis=1, tiled=True)
    u = jnp.concatenate(
        [
            jnp.dot(gathered, streams[j], preferred_element_type=F32).astype(BF16)
            for j in range(3)
        ],
        axis=1,
    )
    edge = from_behind(u[rows - HALO :], "ctx", 1)
    gated = mix(jnp.concatenate([edge, u], axis=0), short_taps, long_taps, skip_gain)
    terms = jnp.dot(gated, w_out, preferred_element_type=F32).astype(BF16)
    return lax.psum_scatter(terms, "tp", scatter_dimension=1, tiled=True)


def solution(mesh):
    in_specs = (
        P("ctx", "tp"),
        P(None, None, "tp"),
        P(None, None, "tp"),
        P(None, "tp"),
        P("tp"),
        P("tp", None),
    )
    out_specs = P("ctx", "tp")
    return jax.shard_map(body, mesh=mesh, in_specs=in_specs, out_specs=out_specs, check_vma=False)
```

time: 460 us -> 351 us (0.76)
  local copies, waits for them, and re-layouts: 157 us -> 0.01 us
  waiting for transfers between devices: 223 us -> 260 us
  Pallas kernels: 0 us -> 26.5 us
  matrix products: 52.7 us -> 43.3 us
    reshape x3 -> x0, local copies, waits for them, and re-layouts: 78.1 us -> none  [the longest x1 45.7 us: toeplitz_blocks(): return spread[:FILT * 2 * FILT].reshape(FILT, 2 * FILT, local)]
    unnamed x13 -> x2, local copies, waits for them, and re-layouts: 35.7 us -> 0.01 us
    all_gather x1, waiting for transfers between devices: 89 us -> 121 us  [body(): gathered = lax.all_gather(tokens, 'tp', axis=1, tiled=True)]
    pallas_call x0 -> x1, Pallas kernels: none -> 26.5 us  [mix(): pl.pallas_call(mix_kernel, out_shape=jax.ShapeDtypeStruct((rows, local),...]
    slice x6 -> x0, local copies, waits for them, and re-layouts: 24.7 us -> none  [the longest x1 22.8 us: toeplitz_blocks(): return spread[:FILT * 2 * FILT].reshape(FILT, 2 * FILT, local)]
    broadcast_in_dim x2 -> x0, local copies, waits for them, and re-layouts: 11.6 us -> none  [the longest x1 11.6 us: toeplitz_blocks(): jnp.broadcast_to(column[None], (FILT, 2 * FILT + 1, local))]
    dot_general x3 -> x4, matrix products: 52.7 us -> 43.3 us  [the longest x3 30.3 us: body(): jnp.dot(gathered, streams[j], preferred_element_type=F32).astype(BF16)]
    ppermute x2 -> x1, waiting for transfers between devices: 5.6 us -> 9.61 us  [from_behind(): lax.ppermute(value, axis, [(source, source + steps) for source in range(f...]
  transfers between devices with their start and end apart: 4 -> 3, of which waited for: 3 -> 3; matrix products, arithmetic and copies ran while one was open for 32% -> 0% of each run, Pallas kernels for 0% -> 0%
where the time goes in v1:
time: 351 us
  waiting for transfers between devices  260 us (74%)
  matrix products  43.3 us (12%)
  Pallas kernels  26.5 us (8%)
  between operations  13.4 us (4%)
  other arithmetic  3.84 us (1%)
  starting transfers between devices  3.62 us (1%)
    reduce_scatter x1, waiting for transfers between devices, body(): return lax.psum_scatter(terms, 'tp', scatter_dimension=1, tiled=True)  128 us
    all_gather x1, waiting for transfers between devices, body(): gathered = lax.all_gather(tokens, 'tp', axis=1, tiled=True)  121 us
    dot_general x3, matrix products, body(): jnp.dot(gathered, streams[j], preferred_element_type=F32).astype(BF16)  30.3 us
    pallas_call x1, Pallas kernels, mix(): pl.pallas_call(mix_kernel, out_shape=jax.ShapeDtypeStruct((rows, local),...  26.5 us
    dot_general x1, matrix products, body(): terms = jnp.dot(gated, w_out, preferred_element_type=F32).astype(BF16)  13 us
    ppermute x1, waiting for transfers between devices, from_behind(): lax.ppermute(value, axis, [(source, source + steps) for source in range(f...  9.61 us
  transfers between devices with their start and end apart: 3, of which 3 were waited for; matrix products, arithmetic and copies ran while one was open for 0% of the time, Pallas kernels for 0%

profile of v1, /device:TPU:0, one launch (start us, length us, event | category | flops | bytes accessed | tf_op | source)
XLA Modules:
  0.0 350.7 jit_solution(14155712204625406748)
XLA Ops:
  6.5 0.0 all-gather.2.cloned.1.call-start
  6.5 0.7 all-gather.2.cloned.1.call-update
  7.3 0.0 reduce-scatter.2.cloned.1.call-start
  7.3 121.1 %all-gather.2.cloned.1.call-done = bf16[768,8192]{1,0:T(8,128)(2,1)} async-done(((bf16[768,1024]{1,0:T(8,128)(2,1)}), bf16[768,8192]{1,0:T(8,128)(2,1)}) %all-gather.2.cloned.1.call-update) | async-done | bytes 12582928 | tf_op jit(solution)/shard_map/all_gather | solution.py:98
  128.4 0.0 copy-start
  128.4 12.2 %fusion.5 = bf16[768,512]{1,0:T(8,128)(2,1)S(1)} fusion(bf16[768,8192]{1,0:T(8,128)(2,1)} %all-gather.2.cloned.1.call-done, bf16[3,8192,512]{2,1,0:T(8,128)(2,1)} %bitcast.23), kind=kOutput, calls=%fused_computation.10 | convolution fusion | flops 6442844160 | bytes 21757952 | tf_op jit(solution)/shard_map/dot_general | solution.py:101
  140.6 0.0 copy-done
  140.6 9.0 %fusion.4 = bf16[768,512]{1,0:T(8,128)(2,1)S(1)} fusion(bf16[768,8192]{1,0:T(8,128)(2,1)S(1)} %copy-done, bf16[3,8192,512]{2,1,0:T(8,128)(2,1)} %bitcast.24), kind=kOutput, calls=%fused_computation.9 | convolution fusion | flops 6442844160 | bytes 21757952 | tf_op jit(solution)/shard_map/dot_general | solution.py:101
  149.6 9.0 %fusion.3 = bf16[768,512]{1,0:T(8,128)(2,1)S(1)} fusion(bf16[768,8192]{1,0:T(8,128)(2,1)S(1)} %copy-done, bf16[3,8192,512]{2,1,0:T(8,128)(2,1)} %bitcast.25), kind=kOutput, calls=%fused_computation.8 | convolution fusion | flops 6442844160 | bytes 21757952 | tf_op jit(solution)/shard_map/dot_general | solution.py:101
  158.7 3.6 %collective-permute-start = (bf16[144,1536]{1,0:T(8,128)(2,1)S(1)}, bf16[144,1536]{1,0:T(8,128)(2,1)S(1)}, u32[]{:S(2)}, u32[]{:S(2)}) collective-permute-start(bf16[144,1536]{1,0:T(8,128)(2,1)S(1)} %pad_maximum_fusion), channel_id=1, source_target_pairs={{0,8},{8,16},{16,24},{1,9},{9,17},{17,25},{2,10},{10,18},{18,26},{... | collective-permute-start | bytes 1327112 | tf_op jit(solution)/shard_map/ppermute | solution.py:19
  162.3 9.6 %collective-permute-done = bf16[144,1536]{1,0:T(8,128)(2,1)S(1)} collective-permute-done((bf16[144,1536]{1,0:T(8,128)(2,1)S(1)}, bf16[144,1536]{1,0:T(8,128)(2,1)S(1)}, u32[]{:S(2)}, u32[]{:S(2)}) %collective-permute-start) | collective-permute-done | bytes 442400 | tf_op jit(solution)/shard_map/ppermute | solution.py:19
  171.9 3.8 %maximum_maximum_fusion.u0.u1.u2 = bf16[912,1536]{1,0:T(8,128)(2,1)} fusion(bf16[768,512]{1,0:T(8,128)(2,1)S(1)} %fusion.5, bf16[768,512]{1,0:T(8,128)(2,1)S(1)} %fusion.4, bf16[768,512]{1,0:T(8,128)(2,1)S(1)} %fusion.3, bf16[144,1536]{1,0:T(8,128)(2,1)S(1)} %collective-permute-done), kind=kLoop, calls=%fused_computation.7 | loop fusion | flops 11206656 | bytes 5603328 | tf_op jit(solution)/shard_map/concatenate | solution.py:107
  175.8 26.5 %mix.1 = bf16[768,512]{1,0:T(8,128)(2,1)} custom-call(bf16[912,1536]{1,0:T(8,128)(2,1)} %maximum_maximum_fusion.u0.u1.u2, bf16[912,1536]{1,0:T(8,128)(2,1)} %maximum_maximum_fusion.u0.u1.u2, bf16[912,1536]{1,0:T(8,128)(2,1)} %maximum_maximum_fusion.u0.u1.u2, bf16[3,3,512]{2,1,0:T(4,128)(2,1)} %short_ref.1, bf16[128,512]{1,0:T(8,128)(2,1)} %long_ref.1, ...), custom_call_target="tpu_custom_call" | custom-call | flops 117964800 | bytes 3145728 | tf_op jit(solution)/shard_map/mix/pallas_call | solution.py:70
  202.3 13.0 %convolution_convert_fusion = bf16[768,8192]{1,0:T(8,128)(2,1)} fusion(bf16[768,512]{1,0:T(8,128)(2,1)} %mix.1, bf16[512,8192]{1,0:T(8,128)(2,1)} %param.11), kind=kOutput, calls=%fused_computation | convolution fusion | flops 6448742400 | bytes 21757952 | tf_op jit(solution)/shard_map/dot_general | solution.py:108
  215.3 0.0 reduce-scatter.2.cloned.1.call-update
  215.3 128.5 %reduce-scatter.2.cloned.1.call-done = bf16[768,1024]{1,0:T(8,128)(2,1)} async-done(((bf16[768,8192]{1,0:T(8,128)(2,1)}), bf16[768,1024]{1,0:T(8,128)(2,1)}) %reduce-scatter.2.cloned.1.call-update) | async-done | bytes 1572880 | tf_op jit(solution)/shard_map/reduce_scatter | solution.py:109
  (1 shorter events, 0.0 us)
Async XLA Ops:
  6.5 121.9 %all-gather.2.cloned.1.call-start = ((), (), s32[]{:S(2)}) async-start(), calls=%async_computation.1 | async-start | bytes 14155776 | tf_op jit(solution)/shard_map/all_gather | solution.py:98
  7.3 336.6 %reduce-scatter.2.cloned.1.call-start = ((), (), s32[]{:S(2)}) async-start(), calls=%async_computation.2 | async-start | bytes 14155776 | tf_op jit(solution)/shard_map/reduce_scatter | solution.py:109
  128.4 12.2 %copy-start = (bf16[768,8192]{1,0:T(8,128)(2,1)S(1)}, bf16[768,8192]{1,0:T(8,128)(2,1)}, u32[]{:S(2)}) copy-start(bf16[768,8192]{1,0:T(8,128)(2,1)} %all-gather.2.cloned.1.call-done) | copy-start | bytes 37748740
  158.7 13.2 %collective-permute-start = (bf16[144,1536]{1,0:T(8,128)(2,1)S(1)}, bf16[144,1536]{1,0:T(8,128)(2,1)S(1)}, u32[]{:S(2)}, u32[]{:S(2)}) collective-permute-start(bf16[144,1536]{1,0:T(8,128)(2,1)S(1)} %pad_maximum_fusion), channel_id=1, source_target_pairs={{0,8},{8,16},{16,24},{1,9},{9,17},{17,25},{2,10},{10,18},{18,26},{... | collective-permute-start | bytes 1327112 | tf_op jit(solution)/shard_map/ppermute | solution.py:19
Sparse Core Ops, SparseCore 0:
  8.9 119.4 all-gather.1
  215.5 128.3 reduce-scatter.1
